TPU v7x, 512 devices: a whole 4x4x16 slice. The times are simulated.
512 devices in a mesh: section: 16 (over z), expert: 32 (over x, y, core).
Axes of the slice: x: 4, y: 4, z: 16, core: 2. Of those that a mesh axis runs over, the one named last changes fastest.
Arguments:
- tokens_in: bfloat16 [16, 512, 4096], P('section', 'expert'), may hold values from -6 to 6
- out_grad: bfloat16 [16, 512, 4096], P('section', 'expert'), may hold values from -6 to 6
- expert_ids: int32 [16, 512, 2], P('section', 'expert'), may hold values from 0 to 7, all different within a row; in each aligned block of 16 rows (0 to 15, 16 to 31, ..., all dimensions but the last counted through in order) at most 8 rows name the same one
- gate_weights: bfloat16 [16, 512, 2], P('section', 'expert'), may hold values from 0.099609375 to 1
- w_gate: bfloat16 [16, 6144, 4096], P('section', 'expert'), may hold values from -0.09375 to 0.09375
- w_up: bfloat16 [16, 6144, 4096], P('section', 'expert'), may hold values from -0.09375 to 0.09375
- w_down: bfloat16 [16, 6144, 4096], P('section', 'expert'), may hold values from -0.09375 to 0.09375
Outputs:
- passed_grad: bfloat16 [16, 512, 4096], P('section', 'expert')
- route_grad: float32 [16, 512, 2], P('section', 'expert')
Inputs may be any that keep to these rules, and one draw needn't show every extreme that they name: `expert_ids`: the 2 experts of a token differ. Among the 16 tokens of one device no expert is named by more than 8 tokens, and in some device's rows some expert is named by exactly 8.
All inputs are finite; a program needn't handle non-finite values.
Results may differ from a plain program's by a relative error of at most 0.0057.
Values may be sent and summed in bfloat16 or wider, within the bound.
A program may use at most 64 MiB of HBM per device.

v0:
```python
import jax
import jax.numpy as jnp
from jax import lax
from jax.sharding import PartitionSpec as P

EXPERTS = 8


def shifted(array, axis, by):
    peers = lax.axis_size(axis)
    return lax.ppermute(array, axis, [(i, (i + by) % peers) for i in range(peers)])


def expert_terms(rows_x, rows_dy, rows_g, gate_mat, up_mat, down_mat):
    dims = (((1,), (1,)), ((), ()))
    gate_pre = lax.dot_general(rows_x, gate_mat, dims, preferred_element_type=jnp.float32)
    up_pre = lax.dot_general(rows_x, up_mat, dims, preferred_element_type=jnp.float32)
    hidden_grad = lax.dot_general(rows_dy, down_mat, dims, preferred_element_type=jnp.float32)
    sigmoid_val = jax.nn.sigmoid(gate_pre)
    activated = gate_pre * sigmoid_val
    slope = sigmoid_val * (1.0 + gate_pre * (1.0 - sigmoid_val))
    scores = jnp.sum(activated * up_pre * hidden_grad, axis=1)
    scaled = hidden_grad * rows_g[:, None]
    grad_gate = (scaled * up_pre * slope).astype(jnp.bfloat16)
    grad_up = (scaled * activated).astype(jnp.bfloat16)
    partial_value = jnp.dot(grad_gate, gate_mat, preferred_element_type=jnp.float32)
    partial_value = partial_value + jnp.dot(grad_up, up_mat, preferred_element_type=jnp.float32)
    return (partial_value.astype(jnp.bfloat16), scores)


def on_device(tokens_in, out_grad, expert_ids, gate_weights, w_gate, w_up, w_down):
    inputs = tokens_in[0]
    upstream = out_grad[0]
    routes = expert_ids[0]
    gate_vals = gate_weights[0]
    gate_mat = w_gate[0]
    up_mat = w_up[0]
    down_mat = w_down[0]
    tok_rows = inputs.shape[0]
    devices = lax.axis_size("expert")
    group_size = devices // EXPERTS
    own_expert = lax.axis_index("expert") // group_size
    route_hit = (routes[:, :, None] == jnp.arange(EXPERTS, dtype=jnp.int32)[None, None, :]).astype(
        jnp.float32
    )
    table = jnp.sum(gate_vals.astype(jnp.float32)[:, :, None] * route_hit, axis=1).astype(
        jnp.bfloat16
    )
    all_x, all_dy, all_table = (
        lax.all_gather(inputs, "expert", axis=0, tiled=True),
        lax.all_gather(upstream, "expert", axis=0, tiled=True),
        lax.all_gather(table, "expert", axis=0, tiled=True),
    )
    picker = (jnp.arange(EXPERTS, dtype=jnp.int32) == own_expert).astype(jnp.float32)
    rows_g = jnp.sum(all_table.astype(jnp.float32) * picker[None, :], axis=1)
    partial_value, scores = expert_terms(all_x, all_dy, rows_g, gate_mat, up_mat, down_mat)
    returned = lax.all_to_all(
        partial_value.reshape(devices, tok_rows, partial_value.shape[1]),
        "expert",
        split_axis=0,
        concat_axis=0,
        tiled=True,
    )
    input_grad = jnp.sum(returned, axis=0, dtype=jnp.float32)
    score_table = lax.psum_scatter(
        scores[:, None] * picker[None, :], "expert", scatter_dimension=0, tiled=True
    )
    grads_route = jnp.sum(route_hit * score_table[:, None, :], axis=2)
    passed = shifted(input_grad.astype(jnp.bfloat16), "section", -1)
    return (passed[None], grads_route[None])


def solution(mesh):
    return jax.shard_map(
        on_device,
        mesh=mesh,
        in_specs=(
            P("section", "expert", None),
            P("section", "expert", None),
            P("section", "expert", None),
            P("section", "expert", None),
            P("section", "expert", None),
            P("section", "expert", None),
            P("section", "expert", None),
        ),
        out_specs=(P("section", "expert", None), P("section", "expert", None)),
        check_vma=False,
    )
```

profile of v0, /device:TPU:1, one launch (start us, length us, event | category | flops | bytes accessed | tf_op | source)
XLA Modules:
  0.0 349.2 jit_solution(10260032153226669373)
XLA Ops:
  7.2 0.0 copy-start
  7.2 0.0 copy-start.1
  7.2 0.0 all-gather.8.cloned.1.call-start
  7.2 0.7 all-gather.8.cloned.1.call-update
  7.9 0.0 all-gather.6.cloned.1.call-start
  8.0 0.7 all-gather.6.cloned.1.call-update
  8.7 0.0 reduce-scatter.4.cloned.1.call-start
  8.7 69.4 %all-gather.8.cloned.1.call-done = bf16[1,512,4096]{2,1,0:T(8,128)(2,1)} async-done(((bf16[1,16,4096]{2,1,0:T(8,128)(2,1)}), bf16[1,512,4096]{2,1,0:T(8,128)(2,1)}) %all-gather.8.cloned.1.call-update) | async-done | bytes 4194320 | tf_op jit(solution)/shard_map/all_gather | solution.py:50
  78.2 0.0 copy-done
  78.2 0.0 copy-start.5
  78.2 3.9 %fusion = f32[512,192]{0,1:T(8,128)S(1)} fusion(bf16[1,512,4096]{2,1,0:T(8,128)(2,1)} %all-gather.8.cloned.1.call-done, bf16[1,192,4096]{2,1,0:T(8,128)(2,1)S(1)} %copy-done), kind=kOutput, calls=%fused_computation.1 | convolution fusion | flops 805306368 | bytes 6160384 | tf_op jit(solution)/shard_map/dot_general | solution.py:16
  82.1 0.0 copy-done.1
  82.1 0.0 copy-done.5
  82.1 2.4 fusion.2
  84.5 0.0 copy-start.6
  84.5 0.0 copy-start.4
  84.5 0.0 copy-start.3
  84.5 57.7 %all-gather.6.cloned.1.call-done = bf16[1,512,4096]{2,1,0:T(8,128)(2,1)} async-done(((bf16[1,16,4096]{2,1,0:T(8,128)(2,1)}), bf16[1,512,4096]{2,1,0:T(8,128)(2,1)}) %all-gather.6.cloned.1.call-update) | async-done | bytes 4194320 | tf_op jit(solution)/shard_map/all_gather | solution.py:51
  142.2 4.2 %multiply_reduce_fusion = (f32[512]{0:T(512)S(1)}, f32[512,192]{0,1:T(8,128)S(1)}) fusion(f32[512,192]{0,1:T(8,128)} %fusion.2, f32[512,192]{0,1:T(8,128)S(1)} %fusion, bf16[1,192,4096]{2,1,0:T(8,128)(2,1)} %param.13, bf16[1,512,4096]{2,1,0:T(8,128)(2,1)} %all-gather.6.cloned.1.call-done), kind=kOutput, calls=%fused_computation.13 | convolution fusion | flops 805993984 | bytes 6948864 | tf_op jit(solution)/shard_map/dot_general | solution.py:18
  146.4 0.1 broadcast_multiply_fusion
  146.5 0.8 copy.22
  147.3 0.0 reduce-scatter.4.cloned.1.call-update
  147.4 0.0 copy-done.6
  147.4 97.7 %reduce-scatter.4.cloned.1.call-done = f32[16,8]{1,0:T(8,128)} async-done(((f32[512,8]{1,0:T(8,128)}), f32[16,8]{1,0:T(8,128)}) %reduce-scatter.4.cloned.1.call-update) | async-done | bytes 528
  245.1 0.8 copy.23
  245.8 0.0 copy-done.4
  245.9 0.6 select_reduce_fusion
  246.4 26.1 %all-gather.2 = bf16[32,16,8]{1,2,0:T(8,128)(2,1)S(1)} all-gather(bf16[1,16,8]{1,2,0:T(8,128)(2,1)S(1)} %bitcast.40), channel_id=1, replica_groups=mesh['section'=16,'expert'=32] {'expert'}, dimensions={0}, use_global_device_ids=true | all-gather | bytes 8448 | tf_op jit(solution)/shard_map/all_gather | solution.py:52
  272.5 0.1 copy.20
  272.6 0.1 copy.21
  272.7 0.1 reshape.29
  272.9 0.1 multiply_reduce_fusion.1
  272.9 0.0 copy-done.3
  272.9 0.0 copy-start.2
  272.9 1.4 fusion.6
  274.3 0.0 copy-done.2
  274.4 1.3 add_convert_fusion
  275.7 55.1 %all_to_all.5 = bf16[32,16,4096]{2,1,0:T(8,128)(2,1)} all-to-all(bf16[32,16,4096]{2,1,0:T(8,128)(2,1)S(1)} %bitcast.38), channel_id=1, replica_groups=mesh['section'=16,'expert'=32] {'expert'}, dimensions={0} | all-to-all | bytes 8388608 | tf_op jit(solution)/shard_map/all_to_all | solution.py:57
  330.8 2.8 reduce_sum.50
  333.6 5.7 %collective-permute-start = (bf16[16,4096]{1,0:T(8,128)(2,1)S(1)}, bf16[16,4096]{1,0:T(8,128)(2,1)S(1)}, u32[]{:S(2)}, u32[]{:S(2)}) collective-permute-start(bf16[16,4096]{1,0:T(8,128)(2,1)S(1)} %reduce_sum.50), channel_id=1, source_target_pairs={{0,480},{32,0},{64,32},{96,64},{128,96},{160,128},{192,160},{224,1... | collective-permute-start | bytes 393224 | tf_op jit(solution)/shard_map/ppermute | solution.py:11
  339.3 2.7 collective-permute-done
  342.0 0.7 copy.25
  (2 shorter events, 0.0 us)
Async XLA Ops:
  7.2 71.0 %copy-start = (bf16[1,192,4096]{2,1,0:T(8,128)(2,1)S(1)}, bf16[1,192,4096]{2,1,0:T(8,128)(2,1)}, u32[]{:S(2)}) copy-start(bf16[1,192,4096]{2,1,0:T(8,128)(2,1)} %param.11) | copy-start | bytes 4718596
  7.2 74.9 %copy-start.1 = (bf16[1,192,4096]{2,1,0:T(8,128)(2,1)S(1)}, bf16[1,192,4096]{2,1,0:T(8,128)(2,1)}, u32[]{:S(2)}) copy-start(bf16[1,192,4096]{2,1,0:T(8,128)(2,1)} %param.12) | copy-start | bytes 4718596
  7.2 71.0 %all-gather.8.cloned.1.call-start = ((), (), s32[]{:S(2)}) async-start(), calls=%async_computation.3 | async-start | bytes 4325376 | tf_op jit(solution)/shard_map/all_gather | solution.py:50
  7.9 134.3 %all-gather.6.cloned.1.call-start = ((), (), s32[]{:S(2)}) async-start(), calls=%async_computation.2 | async-start | bytes 4325376 | tf_op jit(solution)/shard_map/all_gather | solution.py:51
  8.7 236.4 %reduce-scatter.4.cloned.1.call-start = ((), (), s32[]{:S(2)}) async-start(), calls=%async_computation.4 | async-start | bytes 270336
  78.2 3.9 %copy-start.5 = (bf16[1,512,4096]{2,1,0:T(8,128)(2,1)S(1)}, bf16[1,512,4096]{2,1,0:T(8,128)(2,1)}, u32[]{:S(2)}) copy-start(bf16[1,512,4096]{2,1,0:T(8,128)(2,1)} %all-gather.8.cloned.1.call-done) | copy-start | bytes 12582916
  84.5 62.9 %copy-start.6 = (bf16[1,16,2]{1,2,0:T(2,128)(2,1)S(1)}, bf16[1,16,2]{1,2,0:T(2,128)(2,1)}, u32[]{:S(2)}) copy-start(bf16[1,16,2]{1,2,0:T(2,128)(2,1)} %param.10) | copy-start | bytes 196
  84.5 161.4 %copy-start.4 = (s32[1,16,2]{1,2,0:T(2,128)S(1)}, s32[1,16,2]{1,2,0:T(2,128)}, u32[]{:S(2)}) copy-start(s32[1,16,2]{1,2,0:T(2,128)} %param.9) | copy-start | bytes 388
  84.5 188.5 %copy-start.3 = (f32[512,192]{0,1:T(8,128)S(1)}, f32[512,192]{0,1:T(8,128)}, u32[]{:S(2)}) copy-start(f32[512,192]{0,1:T(8,128)} %fusion.2) | copy-start | bytes 1179652
  272.9 1.4 copy-start.2
  333.6 8.4 %collective-permute-start = (bf16[16,4096]{1,0:T(8,128)(2,1)S(1)}, bf16[16,4096]{1,0:T(8,128)(2,1)S(1)}, u32[]{:S(2)}, u32[]{:S(2)}) collective-permute-start(bf16[16,4096]{1,0:T(8,128)(2,1)S(1)} %reduce_sum.50), channel_id=1, source_target_pairs={{0,480},{32,0},{64,32},{96,64},{128,96},{160,128},{192,160},{224,1... | collective-permute-start | bytes 393224 | tf_op jit(solution)/shard_map/ppermute | solution.py:11
Sparse Core Ops, SparseCore 0:
  11.1 67.0 all-gather.7
  81.3 60.8 all-gather.5
  147.5 97.5 reduce-scatter.3
where the time goes:
time: 350 us; the launch traced here: 349 us
  waiting for transfers between devices  229 us (65%)
  blocking collectives  81.1 us (23%)
  between operations  13.9 us (4%)
  matrix products  13.2 us (4%)
  starting transfers between devices  5.82 us (2%)
  other arithmetic  3.58 us (1%)
    unnamed x4, waiting for transfers between devices  99.1 us
    all_gather x1, waiting for transfers between devices, on_device(): lax.all_gather(inputs, 'expert', axis=0, tiled=True)  69.4 us
    all_gather x1, waiting for transfers between devices, on_device(): lax.all_gather(upstream, 'expert', axis=0, tiled=True)  57.7 us
    all_to_all x1, blocking collectives, on_device(): lax.all_to_all(partial_value.reshape(devices, tok_rows, partial_value.sha...  55.1 us
    all_gather x1, blocking collectives, on_device(): lax.all_gather(table, 'expert', axis=0, tiled=True)  26.1 us
  transfers between devices with their start and end apart: 4, of which 4 were waited for; matrix products, arithmetic and copies ran while one was open for 2% of the time, Pallas kernels for 0%

commit v1 on v0

v1 whole, which is shorter than its diff:
```python
import jax
import jax.numpy as jnp
from jax import lax
from jax.experimental import pallas as pl
from jax.experimental.pallas import tpu as pltpu
from jax.sharding import PartitionSpec as P

MESH = pl.DeviceIdType.MESH
BF = jnp.bfloat16
F32 = jnp.float32
NT = (((1,), (1,)), ((), ()))
EXPERTS = 8
Q = 8
LANES = 128
COPIES = 40


def iota(shape, dim):
    return lax.broadcasted_iota(jnp.int32, shape, dim)


def dot_nt(left, right):
    return lax.dot_general(left, right, NT, preferred_element_type=F32)


def resplit(total):
    high = total.astype(BF).astype(F32)
    lane = iota(total.shape, 1)
    return jnp.where(lane < 64, high, total - high).astype(BF)


def kernel(
    x_in, dy_in, ids_in, gw_in, wg_in, wu_in, wd_in, out, route,
    blk, sel, xin, relx, reld, w1, w2, acc, acd, res, rr, rela, relb,
    tb, own, from_m, from_p, add_a, add_b, fin, send, recv, local,
):
    D = x_in.shape[2]
    W = wg_in.shape[1]
    half = D // 2
    sec = lax.axis_index("section")
    secs = lax.axis_size("section")
    me = lax.axis_index("expert")
    core = me % 2
    y = (me // 2) % 4
    x = me // 8
    first = core * y + (1 - core) * x
    second = core * x + (1 - core) * y
    step_a = 8 - 6 * core
    step_b = 2 + 6 * core

    def at(pos_a, pos_b):
        return (sec, core + step_a * (pos_a % 4) + step_b * (pos_b % 4))

    a_up, a_dn = at(first + 1, second), at(first + 3, second)
    b_up, b_dn = at(first, second + 1), at(first, second + 3)
    sib = (sec, me + 1 - 2 * core)
    z_dn = ((sec + secs - 1) % secs, me)
    z_up = ((sec + 1) % secs, me)
    own_e = me // 4

    def expert_at(pos_b):
        pos_b = pos_b % 4
        return (1 - core) * (x * 2 + pos_b // 2) + core * (pos_b * 2 + y // 2)

    peers = [expert_at(second + off) for off in (0, 1, 3, 2)]

    def remote(i, src, dst, dev):
        return pltpu.make_async_remote_copy(
            src_ref=src, dst_ref=dst, send_sem=send.at[i], recv_sem=recv.at[i],
            device_id=dev, device_id_type=MESH,
        )

    lo, hi = pl.ds(0, D), pl.ds(D, D + LANES)
    ra, rb = pl.ds(0, half), pl.ds(half, half + LANES)
    r16 = lambda i: pl.ds(16 * i, 16)

    loads = [
        pltpu.make_async_copy(s, d, local.at[i])
        for i, (s, d) in enumerate(
            [
                (x_in.at[0], blk.at[r16(0), lo]),
                (dy_in.at[0], blk.at[r16(0), pl.ds(D, D)]),
                (wg_in.at[0], w1.at[pl.ds(0, W)]),
                (wu_in.at[0], w1.at[pl.ds(2 * W, W)]),
                (wd_in.at[0], w2.at[pl.ds(0, W)]),
            ]
        )
    ]
    for c in loads:
        c.start()

    barrier = pltpu.get_barrier_semaphore()
    for dev in (a_up, a_dn, b_up, b_dn, sib, z_dn, z_up):
        pl.semaphore_signal(barrier, inc=1, device_id=dev, device_id_type=MESH)

    ids = ids_in[0]
    gates = gw_in[0].astype(F32)
    lane16 = iota((16, LANES), 1)
    table = jnp.zeros((16, LANES), F32)
    for k in range(2):
        table = table + jnp.where(lane16 == ids[:, k : k + 1], gates[:, k : k + 1], 0.0)
    blk[r16(0), pl.ds(2 * D, LANES)] = table.astype(BF)

    pl.semaphore_wait(barrier, 7)
    loads[0].wait()
    loads[1].wait()

    up_x = remote(0, blk.at[r16(0), lo], blk.at[r16(1), lo], a_up)
    up_d = remote(1, blk.at[r16(0), hi], blk.at[r16(1), hi], a_up)
    dn_d = remote(2, blk.at[r16(0), hi], blk.at[r16(2), hi], a_dn)
    dn_x = remote(3, blk.at[r16(0), lo], blk.at[r16(2), lo], a_dn)
    fw_x = remote(4, blk.at[r16(1), lo], blk.at[r16(3), lo], a_up)
    fw_d = remote(5, blk.at[r16(2), hi], blk.at[r16(3), hi], a_dn)
    up_x.start()
    dn_d.start()
    up_d.start()
    dn_x.start()
    halves = [
        remote(6, wg_in.at[0], w1.at[pl.ds(W, W)], sib),
        remote(7, wu_in.at[0], w1.at[pl.ds(3 * W, W)], sib),
        remote(8, wd_in.at[0], w2.at[pl.ds(W, W)], sib),
    ]
    for c in halves:
        c.start()
    up_x.wait_recv()
    fw_x.start()
    dn_d.wait_recv()
    fw_d.start()

    def hits(rows):
        return (blk[rows, pl.ds(2 * D, LANES)].astype(F32) > 0.0).astype(BF)

    def ranks(hit):
        n = hit.shape[0]
        r, c = iota((n, n), 0), iota((n, n), 1)
        lower = ((r // 16 == c // 16) & (c < r)).astype(F32).astype(BF)
        return jnp.dot(lower, hit, preferred_element_type=F32).astype(BF)

    def of_peer(index):
        e = jnp.full(index.shape, peers[3], jnp.int32)
        for j in (2, 1, 0):
            e = jnp.where(index == j, peers[j], e)
        return e

    def cut(size, want):
        return max(d for d in range(LANES, want + 1, LANES) if size % d == 0)

    def select(g):
        hit = hits(pl.ds(32 * g, 32))
        rank = ranks(hit)
        row = iota((64, LANES), 0)
        pick = (iota((64, LANES), 1) == of_peer(row // 16)).astype(F32).astype(BF)
        r, c = iota((64, 32), 0), iota((64, 32), 1)
        good = (dot_nt(pick, hit) > 0.5) & (dot_nt(pick, rank) == (r % 8).astype(F32))
        perm = (good & ((r // 8) % 2 == c // 16)).astype(F32).astype(BF)
        width = cut(2 * D + LANES, 1664)

        @pl.loop(0, (2 * D + LANES) // width)
        def _(i):
            cols = pl.ds(pl.multiple_of(i * width, LANES), width)
            got = jnp.dot(
                perm, blk[pl.ds(32 * g, 32), cols], preferred_element_type=F32
            ).astype(BF)
            xin[r16(g), cols] = got[0:16]
            sel[g, :, cols] = got[16:64]

    def direct(g):
        return [
            remote(9 + g, sel.at[g, r16(0)], xin.at[r16(4 + 2 * g)], b_up),
            remote(11 + g, sel.at[g, r16(1)], xin.at[r16(5 + 2 * g)], b_dn),
        ]

    def opposite(g):
        return [
            remote(13 + g, sel.at[g, r16(2), lo], relx.at[g], b_up),
            remote(15 + g, sel.at[g, r16(2), hi], reld.at[g], b_dn),
        ]

    def onward(g):
        return [
            remote(17 + g, relx.at[g], xin.at[r16(2 + g), lo], b_up),
            remote(19 + g, reld.at[g], xin.at[r16(2 + g), hi], b_dn),
        ]

    def go(copies):
        for c in copies:
            c.start()

    def arrived(copies):
        for c in copies:
            c.wait_recv()

    up_d.wait_recv()
    select(0)
    go(opposite(0))
    go(direct(0))
    dn_x.wait_recv()
    fw_x.wait_recv()
    fw_d.wait_recv()
    select(1)
    go(opposite(1))

    hit = hits(pl.ds(0, 64))
    rank = ranks(hit)
    row = iota((LANES, LANES), 0)
    pick = (iota((LANES, LANES), 1) == of_peer(row // 32)).astype(F32).astype(BF)
    r, c = iota((64, LANES), 0), iota((64, LANES), 1)
    good = (dot_nt(hit, pick) > 0.5) & (dot_nt(rank, pick) == (c % 8).astype(F32))
    place = (good & ((c // 8) % 4 == r // 16)).astype(F32).astype(BF)

    for c, f in zip(opposite(0), onward(0)):
        c.wait_recv()
        f.start()

    def experts(row0, count, dst, middle):
        rows = pl.ds(row0, count)
        depth = 512 if D % 512 == 0 else LANES
        acc[0:count] = jnp.zeros((count, 4 * W), F32)
        acd[0:count] = jnp.zeros((count, 2 * W), F32)

        @pl.loop(0, D // depth)
        def _(k):
            cols = pl.ds(pl.multiple_of(k * depth, LANES), depth)
            cols_d = pl.ds(pl.multiple_of(D + k * depth, LANES), depth)
            acc[0:count] += dot_nt(xin[rows, cols], w1[:, cols])
            acd[0:count] += dot_nt(xin[rows, cols_d], w2[:, cols])

        gate_pre = acc[0:count, 0 : 2 * W]
        up_pre = acc[0:count, 2 * W : 4 * W]
        hidden = acd[0:count]
        side = xin[rows, pl.ds(2 * D, LANES)].astype(F32)
        lane = iota((count, LANES), 1)
        gate = jnp.sum(jnp.where(lane == own_e, side, 0.0), axis=1, keepdims=True)
        sig = jax.nn.sigmoid(gate_pre)
        act = gate_pre * sig
        slope = sig * (1.0 + gate_pre * (1.0 - sig))
        score = jnp.sum(act * up_pre * hidden, axis=1, keepdims=True)
        scaled = hidden * gate
        grads = jnp.concatenate(
            [(scaled * up_pre * slope).astype(BF), (scaled * act).astype(BF)], axis=1
        )
        middle()
        base = 0 if dst is rr else row0

        @pl.loop(0, D // depth)
        def _(k):
            cols = pl.ds(pl.multiple_of(k * depth, LANES), depth)
            dst[pl.ds(base, count), cols] = jnp.dot(
                grads, w1[:, cols], preferred_element_type=F32
            ).astype(BF)

        mine = (lane % 64) == own_e
        dst[pl.ds(base, count), pl.ds(D, LANES)] = resplit(jnp.where(mine, score, 0.0))

    def nothing():
        return None

    for c in loads[2:]:
        c.wait()
    for c in halves:
        c.wait_recv()
    experts(0, 32, rr, nothing)
    for c, f in zip(opposite(1), onward(1)):
        c.wait_recv()
        f.start()
    go(direct(1))
    arrived(onward(0) + onward(1) + direct(0))
    experts(32, 64, res, nothing)

    back_opp = [
        remote(21, res.at[pl.ds(32, 32), ra], rela, b_up),
        remote(22, res.at[pl.ds(32, 32), rb], relb, b_dn),
    ]
    back_fw = [
        remote(23, rela, rr.at[pl.ds(96, 32), ra], b_up),
        remote(24, relb, rr.at[pl.ds(96, 32), rb], b_dn),
    ]

    def back(g):
        return [
            remote(25 + g, res.at[r16(4 + 2 * g)], rr.at[r16(2 + g)], b_dn),
            remote(27 + g, res.at[r16(5 + 2 * g)], rr.at[r16(4 + g)], b_up),
        ]

    go(back_opp)
    go(back(0))
    arrived(direct(1))

    def relay():
        for c, f in zip(back_opp, back_fw):
            c.wait_recv()
            f.start()

    experts(96, 32, res, relay)
    go(back(1))
    arrived(back(0) + back_fw + back(1))

    width = cut(D, 512)

    @pl.loop(0, D // width)
    def _(i):
        cols = pl.ds(pl.multiple_of(i * width, LANES), width)
        got = jnp.dot(place, rr[:, cols], preferred_element_type=F32)
        own[:, cols] = got[0:16]
        tb[:, cols] = got[16:64].astype(BF)

    swap = lambda v: pltpu.roll(v, 64, 1)
    cols_s = pl.ds(D, LANES)
    got = jnp.dot(place, rr[:, cols_s], preferred_element_type=F32)
    got = resplit(got + swap(got)).astype(F32)
    own[:, cols_s] = got[0:16]
    tb[:, cols_s] = got[16:64].astype(BF)

    opp_a = remote(29, tb.at[r16(2), ra], add_a, a_up)
    opp_b = remote(30, tb.at[r16(2), rb], add_b, a_dn)
    plain_b = remote(31, tb.at[r16(1), rb], from_m.at[:, rb], a_up)
    plain_a = remote(32, tb.at[r16(0), ra], from_p.at[:, ra], a_dn)
    summed_a = remote(33, fin.at[0, :, ra], from_m.at[:, ra], a_up)
    summed_b = remote(34, fin.at[0, :, rb], from_p.at[:, rb], a_dn)
    go([opp_a, opp_b, plain_b, plain_a])
    opp_a.wait_recv()
    fin[0, :, ra] = (tb[r16(1), ra].astype(F32) + add_a[...].astype(F32)).astype(BF)
    summed_a.start()
    opp_b.wait_recv()
    rm = pl.ds(half, half)
    fin[0, :, rm] = (
        tb[r16(0), rm].astype(F32) + add_b[:, 0:half].astype(F32)
    ).astype(BF)
    got = tb[r16(0), cols_s].astype(F32) + add_b[:, half : half + LANES].astype(F32)
    fin[0, :, cols_s] = resplit(got + swap(got))
    summed_b.start()

    last_a = remote(35, fin.at[1, :, ra], out.at[0, :, ra], z_dn)
    last_b = remote(36, fin.at[1, :, rm], out.at[0, :, rm], z_dn)
    arrived([plain_a, summed_a])
    fin[1, :, ra] = (
        own[:, ra] + from_m[:, ra].astype(F32) + from_p[:, ra].astype(F32)
    ).astype(BF)
    last_a.start()
    arrived([plain_b, summed_b])
    fin[1, :, rm] = (
        own[:, rm] + from_m[:, rm].astype(F32) + from_p[:, rm].astype(F32)
    ).astype(BF)
    last_b.start()
    got = own[:, cols_s] + from_m[:, cols_s].astype(F32) + from_p[:, cols_s].astype(F32)
    got = got + swap(got)
    route[0] = jnp.concatenate(
        [
            jnp.sum(jnp.where(lane16 == ids[:, k : k + 1], got, 0.0), axis=1, keepdims=True)
            for k in range(2)
        ],
        axis=1,
    )

    every = [up_x, up_d, dn_d, dn_x, fw_x, fw_d] + halves
    for g in range(2):
        every = every + direct(g) + opposite(g) + onward(g) + back(g)
    every = every + back_opp + back_fw
    every = every + [opp_a, opp_b, plain_a, plain_b, summed_a, summed_b, last_a, last_b]
    for c in every:
        c.wait_send()
    arrived([last_a, last_b])


def on_device(tokens_in, out_grad, expert_ids, gate_weights, w_gate, w_up, w_down):
    D = tokens_in.shape[2]
    W = w_gate.shape[1]
    wide, back, half = 2 * D + LANES, D + LANES, D // 2
    hbm = pl.BlockSpec(memory_space=pl.ANY)
    vmem = pl.BlockSpec(memory_space=pltpu.VMEM)
    return pl.pallas_call(
        kernel,
        out_shape=(
            jax.ShapeDtypeStruct(tokens_in.shape, BF),
            jax.ShapeDtypeStruct(expert_ids.shape, F32),
        ),
        in_specs=[hbm, hbm, vmem, vmem, hbm, hbm, hbm],
        out_specs=(hbm, vmem),
        scratch_shapes=[
            pltpu.VMEM((64, wide), BF),
            pltpu.VMEM((2, 48, wide), BF),
            pltpu.VMEM((128, wide), BF),
            pltpu.VMEM((2, 16, D), BF),
            pltpu.VMEM((2, 16, D + LANES), BF),
            pltpu.VMEM((4 * W, D), BF),
            pltpu.VMEM((2 * W, D), BF),
            pltpu.VMEM((64, 4 * W), F32),
            pltpu.VMEM((64, 2 * W), F32),
            pltpu.VMEM((128, back), BF),
            pltpu.VMEM((128, back), BF),
            pltpu.VMEM((32, half), BF),
            pltpu.VMEM((32, half + LANES), BF),
            pltpu.VMEM((48, back), BF),
            pltpu.VMEM((16, back), F32),
            pltpu.VMEM((16, back), BF),
            pltpu.VMEM((16, back), BF),
            pltpu.VMEM((16, half), BF),
            pltpu.VMEM((16, half + LANES), BF),
            pltpu.VMEM((2, 16, back), BF),
            pltpu.SemaphoreType.DMA((COPIES,)),
            pltpu.SemaphoreType.DMA((COPIES,)),
            pltpu.SemaphoreType.DMA((5,)),
        ],
        compiler_params=pltpu.CompilerParams(collective_id=0, has_side_effects=True),
    )(tokens_in, out_grad, expert_ids, gate_weights, w_gate, w_up, w_down)


def solution(mesh):
    spec = P("section", "expert", None)
    return jax.shard_map(
        on_device, mesh=mesh, in_specs=(spec,) * 7, out_specs=(spec, spec), check_vma=False
    )
```

time: 350 us -> 72.7 us (0.21)
  the two profiles are of different devices: /device:TPU:1 before, /device:TPU:2 now
where the time goes in v1:
time: 72.7 us; the launch traced here: 72.4 us
  Pallas kernels  66.2 us (91%)
  local copies, waits for them, and re-layouts  5.58 us (8%)
    pallas_call x1, Pallas kernels, on_device(): pl.pallas_call(kernel, out_shape=(jax.ShapeDtypeStruct(tokens_in.shape, B...  66.2 us
    unnamed x3, local copies, waits for them, and re-layouts  4.25 us

profile of v1, /device:TPU:2, one launch (start us, length us, event | category | flops | bytes accessed | tf_op | source)
XLA Modules:
  0.0 72.4 jit_solution(16690582775580423429)
XLA Ops:
  0.6 1.3 %copy.10.gw_in = bf16[1,16,2]{2,1,0:T(8,128)(2,1)} copy(bf16[1,16,2]{1,2,0:T(2,128)(2,1)} %param.10) | data formatting | bytes 128 | tf_op args[3]
  2.0 1.4 %copy.9.ids_in = s32[1,16,2]{2,1,0:T(8,128)} copy(s32[1,16,2]{1,2,0:T(2,128)} %param.9) | data formatting | bytes 256 | tf_op args[2]
  3.3 66.2 %shard_map.86 = (bf16[1,16,4096]{2,1,0:T(8,128)(2,1)}, f32[1,16,2]{2,1,0:T(8,128)}) custom-call(bf16[1,16,4096]{2,1,0:T(8,128)(2,1)} %x_in.1, bf16[1,16,4096]{2,1,0:T(8,128)(2,1)} %dy_in.1, s32[1,16,2]{2,1,0:T(8,128)} %copy.9.ids_in, bf16[1,16,2]{2,1,0:T(8,128)(2,1)} %copy.10.gw_in, bf16[1,192,4096]{2,1,0:T(8,128)(2,1)} %wg_in.1, ...), custom_call_target="tpu_custom_call" | custom-call | tf_op jit(solution)/shard_map/pallas_call | solution.py:371
  69.5 1.3 %copy.11 = f32[1,16,2]{1,2,0:T(2,128)} copy(f32[1,16,2]{2,1,0:T(8,128)} %get-tuple-element.3) | data formatting | bytes 256 | tf_op jit(solution)/shard_map/pallas_call | solution.py:371
  70.9 1.6 %copy.13 = bf16[1,16,4096]{2,1,0:T(8,128)(2,1)} copy(bf16[1,16,4096]{2,1,0:T(8,128)(2,1)} %get-tuple-element.6) | data formatting | bytes 262144

commit v2 on v0

v2 whole, which is shorter than its diff:
```python
import jax
import jax.numpy as jnp
from jax import lax
from jax.experimental import pallas as pl
from jax.experimental.pallas import tpu as pltpu
from jax.sharding import PartitionSpec as P

MESH = pl.DeviceIdType.MESH
BF = jnp.bfloat16
F32 = jnp.float32
NT = (((1,), (1,)), ((), ()))
EXPERTS = 8
Q = 8
LANES = 128
COPIES = 64
PIECES = 4


def iota(shape, dim):
    return lax.broadcasted_iota(jnp.int32, shape, dim)


def ones(mask):
    return mask.astype(F32).astype(BF)


def dot_nt(left, right):
    return lax.dot_general(left, right, NT, preferred_element_type=F32)


def resplit(total):
    high = total.astype(BF).astype(F32)
    lane = iota(total.shape, 1)
    return jnp.where(lane < 64, high, total - high).astype(BF)


def kernel(
    x_in, dy_in, ids_in, gw_in, wg_in, wu_in, wd_in, out, route,
    blk, sel, xin, w1, w2, acc, acd, res, rr, tb, own, parts, fin,
    send, recv, local,
):
    D = x_in.shape[2]
    W = wg_in.shape[1]
    sec = lax.axis_index("section")
    secs = lax.axis_size("section")
    me = lax.axis_index("expert")
    core = me % 2
    y = (me // 2) % 4
    x = me // 8
    first = core * y + (1 - core) * x
    second = core * x + (1 - core) * y
    step_a = 8 - 6 * core
    step_b = 2 + 6 * core

    def at(pos_a, pos_b):
        return (sec, core + step_a * (pos_a % 4) + step_b * (pos_b % 4))

    a_up, a_dn, a_op = [at(first + k, second) for k in (1, 3, 2)]
    b_up, b_dn, b_op = [at(first, second + k) for k in (1, 3, 2)]
    sib = (sec, me + 1 - 2 * core)
    z_dn = ((sec + secs - 1) % secs, me)
    z_up = ((sec + 1) % secs, me)
    own_e = me // 4

    def expert_at(pos_b):
        pos_b = pos_b % 4
        return (1 - core) * (x * 2 + pos_b // 2) + core * (pos_b * 2 + y // 2)

    peers = [expert_at(second + off) for off in (0, 1, 3, 2)]

    flying, landing = {}, {}

    class Push:
        def __init__(self, src, dst, dev):
            self.i = Push.count
            Push.count += 1
            self.copy = pltpu.make_async_remote_copy(
                src_ref=src, dst_ref=dst, send_sem=send.at[self.i],
                recv_sem=recv.at[self.i], device_id=dev, device_id_type=MESH,
            )

        def start(self):
            self.copy.start()
            flying[self.i] = landing[self.i] = self.copy

        def wait(self):
            self.copy.wait_recv()
            landing.pop(self.i)

    Push.count = 0

    def go(copies):
        for c in copies:
            c.start()

    def arrived(copies):
        for c in copies:
            c.wait()

    def finish():
        for c in landing.values():
            c.wait_recv()
        for c in flying.values():
            c.wait_send()

    r16 = lambda i: pl.ds(16 * i, 16)
    side = pl.ds(D, LANES)
    step = D // PIECES
    piece = [
        pl.ds(i * step, step + (LANES if i == PIECES - 1 else 0)) for i in range(PIECES)
    ]

    loads = [
        pltpu.make_async_copy(s, d, local.at[i])
        for i, (s, d) in enumerate(
            [
                (x_in.at[0], blk.at[r16(0), pl.ds(0, D)]),
                (dy_in.at[0], blk.at[r16(0), pl.ds(D, D)]),
                (wg_in.at[0], w1.at[pl.ds(0, W)]),
                (wu_in.at[0], w1.at[pl.ds(2 * W, W)]),
                (wd_in.at[0], w2.at[pl.ds(0, W)]),
            ]
        )
    ]
    for c in loads:
        c.start()

    barrier = pltpu.get_barrier_semaphore()
    around = (a_up, a_dn, a_op, b_up, b_dn, b_op, sib, z_dn, z_up)
    for dev in around:
        pl.semaphore_signal(barrier, inc=1, device_id=dev, device_id_type=MESH)

    ids = ids_in[0]
    gates = gw_in[0].astype(F32)
    eye = ones(iota((16, 16), 0) == iota((16, 16), 1))
    row_e = iota((LANES, 16), 0)
    table = jnp.zeros((LANES, 16), F32)
    for k in range(2):
        table = table + jnp.where(row_e == ids[k : k + 1], gates[k : k + 1], 0.0)
    blk[r16(0), pl.ds(2 * D, LANES)] = dot_nt(eye, table.astype(BF)).astype(BF)

    pl.semaphore_wait(barrier, len(around))
    loads[0].wait()
    loads[1].wait()

    gather = [
        Push(blk.at[r16(0)], blk.at[r16(q)], dev)
        for q, dev in ((1, a_up), (2, a_dn), (3, a_op))
    ]
    go(gather)
    halves = [
        Push(wg_in.at[0], w1.at[pl.ds(W, W)], sib),
        Push(wu_in.at[0], w1.at[pl.ds(3 * W, W)], sib),
        Push(wd_in.at[0], w2.at[pl.ds(W, W)], sib),
    ]
    go(halves)

    def of_peer(index):
        e = jnp.full(index.shape, peers[3], jnp.int32)
        for j in (2, 1, 0):
            e = jnp.where(index == j, peers[j], e)
        return e

    def cut(size, want):
        return max(d for d in range(LANES, want + 1, LANES) if size % d == 0)

    r32, c32 = iota((32, 32), 0), iota((32, 32), 1)
    lower = ones((r32 // 16 == c32 // 16) & (c32 < r32))
    pick = ones(iota((64, LANES), 1) == of_peer(iota((64, LANES), 0) // 16))

    def routing(g):
        hit = ones(blk[pl.ds(32 * g, 32), pl.ds(2 * D, LANES)].astype(F32) > 0.0)
        return hit, jnp.dot(lower, hit, preferred_element_type=F32).astype(BF)

    def select(g):
        hit, rank = routing(g)
        r, c = iota((64, 32), 0), iota((64, 32), 1)
        good = (dot_nt(pick, hit) > 0.5) & (dot_nt(pick, rank) == (r % 8).astype(F32))
        perm = ones(good & ((r // 8) % 2 == c // 16))
        width = cut(2 * D + LANES, 1664)

        @pl.loop(0, (2 * D + LANES) // width)
        def _(i):
            cols = pl.ds(pl.multiple_of(i * width, LANES), width)
            got = jnp.dot(
                perm, blk[pl.ds(32 * g, 32), cols], preferred_element_type=F32
            ).astype(BF)
            xin[r16(4 * g), cols] = got[0:16]
            sel[g, :, cols] = got[16:64]

    def placing(g):
        hit, rank = routing(g)
        r, c = iota((32, 64), 0), iota((32, 64), 1)
        good = (dot_nt(hit, pick) > 0.5) & (dot_nt(rank, pick) == (c % 8).astype(F32))
        return ones(good & ((c // 8) % 2 == r // 16))

    def dispatch(g):
        return [
            [
                Push(sel.at[g, r16(j - 1), cols], xin.at[r16(4 * g + j), cols], dev)
                for j, dev in ((3, b_op), (1, b_up), (2, b_dn))
            ]
            for cols in (pl.ds(0, D), pl.ds(D, D + LANES))
        ]

    sent = [dispatch(0), dispatch(1)]
    back = [
        [
            [
                Push(res.at[g, r16(j - 1), cols], rr.at[r16(4 * g + j), cols], dev)
                for j, dev in ((3, b_op), (1, b_dn), (2, b_up))
            ]
            for cols in piece
        ]
        for g in range(2)
    ]
    reduce = {
        q: [Push(tb.at[r16(q - 1), cols], parts.at[q - 1, :, cols], dev) for cols in piece]
        for q, dev in ((1, a_dn), (2, a_up), (3, a_op))
    }
    last = [
        Push(fin.at[:, pl.ds(i * step, step)], out.at[0, :, pl.ds(i * step, step)], z_dn)
        for i in range(PIECES)
    ]

    gather[0].wait()
    select(0)
    go(sent[0][0] + sent[0][1])
    arrived(gather[1:])
    select(1)
    go(sent[1][0] + sent[1][1])
    place = [placing(0), placing(1)]

    for c in loads[2:]:
        c.wait()
    arrived(halves)
    depth = 512 if D % 512 == 0 else LANES

    def experts(g):
        rows = pl.ds(64 * g, 64)
        acc[...] = jnp.zeros((64, 4 * W), F32)
        acd[...] = jnp.zeros((64, 2 * W), F32)
        arrived(sent[g][0])

        @pl.loop(0, D // depth)
        def _(k):
            cols = pl.ds(pl.multiple_of(k * depth, LANES), depth)
            acc[...] += dot_nt(xin[rows, cols], w1[:, cols])

        arrived(sent[g][1])

        @pl.loop(0, D // depth)
        def _(k):
            cols = pl.ds(pl.multiple_of(k * depth, LANES), depth)
            cols_d = pl.ds(pl.multiple_of(D + k * depth, LANES), depth)
            acd[...] += dot_nt(xin[rows, cols_d], w2[:, cols])

        gate_pre = acc[:, 0 : 2 * W]
        up_pre = acc[:, 2 * W : 4 * W]
        hidden = acd[...]
        lane = iota((64, LANES), 1)
        gate = jnp.sum(
            jnp.where(lane == own_e, xin[rows, pl.ds(2 * D, LANES)].astype(F32), 0.0),
            axis=1, keepdims=True,
        )
        sig = jax.nn.sigmoid(gate_pre)
        act = gate_pre * sig
        slope = sig * (1.0 + gate_pre * (1.0 - sig))
        score = jnp.sum(act * up_pre * hidden, axis=1, keepdims=True)
        scaled = hidden * gate
        grads = jnp.concatenate(
            [(scaled * up_pre * slope).astype(BF), (scaled * act).astype(BF)], axis=1
        )
        scores = resplit(jnp.where((lane % 64) == own_e, score, 0.0))
        rr[r16(4 * g), side] = scores[0:16]
        res[g, :, side] = scores[16:64]
        width = cut(step, 512)
        for i in range(PIECES):

            @pl.loop(0, step // width)
            def _(k):
                cols = pl.ds(pl.multiple_of(i * step + k * width, LANES), width)
                got = jnp.dot(
                    grads, w1[:, cols], preferred_element_type=F32
                ).astype(BF)
                rr[r16(4 * g), cols] = got[0:16]
                res[g, :, cols] = got[16:64]

            go(back[g][i])

    experts(0)
    experts(1)

    swap = lambda v: pltpu.roll(v, 64, 1)
    for g in range(2):
        rows = pl.ds(64 * g, 64)
        for i in range(PIECES):
            arrived(back[g][i])
            cols = pl.ds(i * step, step)
            got = jnp.dot(place[g], rr[rows, cols], preferred_element_type=F32)
            got_s = None
            if i == PIECES - 1:
                got_s = jnp.dot(place[g], rr[rows, side], preferred_element_type=F32)
                got_s = resplit(got_s + swap(got_s))
            if g == 0:
                own[:, cols] = got[0:16]
                tb[r16(0), cols] = got[16:32].astype(BF)
                if got_s is not None:
                    own[:, side] = got_s[0:16].astype(F32)
                    tb[r16(0), side] = got_s[16:32]
                go([reduce[1][i]])
            else:
                tb[pl.ds(16, 32), cols] = got.astype(BF)
                if got_s is not None:
                    tb[pl.ds(16, 32), side] = got_s
                go([reduce[3][i], reduce[2][i]])

    def total(cols):
        got = own[:, cols]
        for q in range(3):
            got = got + parts[q, :, cols].astype(F32)
        return got

    for i in range(PIECES):
        arrived([reduce[q][i] for q in (1, 2, 3)])
        cols = pl.ds(i * step, step)
        fin[:, cols] = total(cols).astype(BF)
        last[i].start()

    got = total(side)
    got = got + swap(got)
    ids_col = dot_nt(eye, ids.astype(F32).astype(BF))
    lane16 = iota((16, LANES), 1).astype(F32)
    for k in range(2):
        col = jnp.sum(
            jnp.where(lane16 == ids_col[:, k : k + 1], got, 0.0), axis=1, keepdims=True
        )
        route[0, k : k + 1, :] = jnp.sum(
            jnp.where(iota((16, 16), 0) == iota((16, 16), 1), col, 0.0),
            axis=0, keepdims=True,
        )
    finish()


def on_device(tokens_in, out_grad, expert_ids, gate_weights, w_gate, w_up, w_down):
    D = tokens_in.shape[2]
    W = w_gate.shape[1]
    wide, back = 2 * D + LANES, D + LANES
    hbm = pl.BlockSpec(memory_space=pl.ANY)
    vmem = pl.BlockSpec(memory_space=pltpu.VMEM)
    ids = jnp.swapaxes(expert_ids, 1, 2)
    grad, route = pl.pallas_call(
        kernel,
        out_shape=(
            jax.ShapeDtypeStruct(tokens_in.shape, BF),
            jax.ShapeDtypeStruct(ids.shape, F32),
        ),
        in_specs=[hbm, hbm, vmem, vmem, hbm, hbm, hbm],
        out_specs=(hbm, vmem),
        scratch_shapes=[
            pltpu.VMEM((64, wide), BF),
            pltpu.VMEM((2, 48, wide), BF),
            pltpu.VMEM((128, wide), BF),
            pltpu.VMEM((4 * W, D), BF),
            pltpu.VMEM((2 * W, D), BF),
            pltpu.VMEM((64, 4 * W), F32),
            pltpu.VMEM((64, 2 * W), F32),
            pltpu.VMEM((2, 48, back), BF),
            pltpu.VMEM((128, back), BF),
            pltpu.VMEM((48, back), BF),
            pltpu.VMEM((16, back), F32),
            pltpu.VMEM((3, 16, back), BF),
            pltpu.VMEM((16, D), BF),
            pltpu.SemaphoreType.DMA((COPIES,)),
            pltpu.SemaphoreType.DMA((COPIES,)),
            pltpu.SemaphoreType.DMA((5,)),
        ],
        compiler_params=pltpu.CompilerParams(collective_id=0, has_side_effects=True),
    )(tokens_in, out_grad, ids, jnp.swapaxes(gate_weights, 1, 2), w_gate, w_up, w_down)
    return grad, jnp.swapaxes(route, 1, 2)


def solution(mesh):
    spec = P("section", "expert", None)
    return jax.shard_map(
        on_device, mesh=mesh, in_specs=(spec,) * 7, out_specs=(spec, spec), check_vma=False
    )
```

time: 350 us -> 57 us (0.16)
  the two profiles are of different devices: /device:TPU:1 before, /device:TPU:2 now
where the time goes in v2:
time: 57 us; the launch traced here: 56.9 us
  Pallas kernels  53.4 us (94%)
  local copies, waits for them, and re-layouts  2.8 us (5%)
  between operations  0.64 us (1%)
    pallas_call x1, Pallas kernels, on_device(): pl.pallas_call(kernel, out_shape=(jax.ShapeDtypeStruct(tokens_in.shape, B...  53.4 us
    unnamed x2, local copies, waits for them, and re-layouts  2.8 us

profile of v2, /device:TPU:2, one launch (start us, length us, event | category | flops | bytes accessed | tf_op | source)
XLA Modules:
  0.0 56.9 jit_solution(5151220189754260000)
XLA Ops:
  0.6 53.4 %shard_map.86 = (bf16[1,16,4096]{2,1,0:T(8,128)(2,1)}, f32[1,2,16]{2,1,0:T(2,128)}) custom-call(bf16[1,16,4096]{2,1,0:T(8,128)(2,1)} %x_in.1, bf16[1,16,4096]{2,1,0:T(8,128)(2,1)} %dy_in.1, s32[1,2,16]{2,1,0:T(2,128)} %bitcast.4, bf16[1,2,16]{2,1,0:T(2,128)(2,1)} %bitcast.5, bf16[1,192,4096]{2,1,0:T(8,128)(2,1)} %wg_in.1, bf16[1,192,4096]{2,1,0:T(8,128)(2,1)} %wu_in.1, ...), custom_call_target="tpu_custom_call" | custom-call | tf_op jit(solution)/shard_map/pallas_call | solution.py:352
  54.1 1.6 %copy.11 = bf16[1,16,4096]{2,1,0:T(8,128)(2,1)} copy(bf16[1,16,4096]{2,1,0:T(8,128)(2,1)} %get-tuple-element.8) | data formatting | bytes 262144
  55.7 1.2 %copy.12 = f32[1,16,2]{1,2,0:T(2,128)} copy(f32[1,16,2]{1,2,0:T(2,128)} %bitcast.3) | data formatting | bytes 256

commit v3 on v2

--- a/solution.py
+++ b/solution.py
@@ -36,7 +36,7 @@
 
 def kernel(
     x_in, dy_in, ids_in, gw_in, wg_in, wu_in, wd_in, out, route,
-    blk, sel, xin, w1, w2, acc, acd, res, rr, tb, own, parts, fin,
+    blk, sel, xin, w1, w2, acc, res, rr, tb, own, parts, fin,
     send, recv, local,
 ):
     D = x_in.shape[2]
@@ -105,6 +105,8 @@
 
     r16 = lambda i: pl.ds(16 * i, 16)
     side = pl.ds(D, LANES)
+    head = pl.ds(0, LANES)
+    parts_in = (pl.ds(0, LANES + D), pl.ds(LANES + D, D))
     step = D // PIECES
     piece = [
         pl.ds(i * step, step + (LANES if i == PIECES - 1 else 0)) for i in range(PIECES)
@@ -114,8 +116,8 @@
         pltpu.make_async_copy(s, d, local.at[i])
         for i, (s, d) in enumerate(
             [
-                (x_in.at[0], blk.at[r16(0), pl.ds(0, D)]),
-                (dy_in.at[0], blk.at[r16(0), pl.ds(D, D)]),
+                (x_in.at[0], blk.at[r16(0), pl.ds(LANES, D)]),
+                (dy_in.at[0], blk.at[r16(0), pl.ds(LANES + D, D)]),
                 (wg_in.at[0], w1.at[pl.ds(0, W)]),
                 (wu_in.at[0], w1.at[pl.ds(2 * W, W)]),
                 (wd_in.at[0], w2.at[pl.ds(0, W)]),
@@ -137,17 +139,21 @@
     table = jnp.zeros((LANES, 16), F32)
     for k in range(2):
         table = table + jnp.where(row_e == ids[k : k + 1], gates[k : k + 1], 0.0)
-    blk[r16(0), pl.ds(2 * D, LANES)] = dot_nt(eye, table.astype(BF)).astype(BF)
+    blk[r16(0), head] = dot_nt(eye, table.astype(BF)).astype(BF)
 
     pl.semaphore_wait(barrier, len(around))
     loads[0].wait()
+
+    gather = [
+        [
+            Push(blk.at[r16(0), cols], blk.at[r16(q), cols], dev)
+            for q, dev in ((1, a_up), (2, a_dn), (3, a_op))
+        ]
+        for cols in parts_in
+    ]
+    go(gather[0][:2])
     loads[1].wait()
-
-    gather = [
-        Push(blk.at[r16(0)], blk.at[r16(q)], dev)
-        for q, dev in ((1, a_up), (2, a_dn), (3, a_op))
-    ]
-    go(gather)
+    go(gather[1][:2] + [gather[0][2], gather[1][2]])
     halves = [
         Push(wg_in.at[0], w1.at[pl.ds(W, W)], sib),
         Push(wu_in.at[0], w1.at[pl.ds(3 * W, W)], sib),
@@ -169,19 +175,22 @@
     pick = ones(iota((64, LANES), 1) == of_peer(iota((64, LANES), 0) // 16))
 
     def routing(g):
-        hit = ones(blk[pl.ds(32 * g, 32), pl.ds(2 * D, LANES)].astype(F32) > 0.0)
+        hit = ones(blk[pl.ds(32 * g, 32), head].astype(F32) > 0.0)
         return hit, jnp.dot(lower, hit, preferred_element_type=F32).astype(BF)
 
-    def select(g):
+    def selection(g):
         hit, rank = routing(g)
         r, c = iota((64, 32), 0), iota((64, 32), 1)
         good = (dot_nt(pick, hit) > 0.5) & (dot_nt(pick, rank) == (r % 8).astype(F32))
-        perm = ones(good & ((r // 8) % 2 == c // 16))
-        width = cut(2 * D + LANES, 1664)
-
-        @pl.loop(0, (2 * D + LANES) // width)
+        return ones(good & ((r // 8) % 2 == c // 16))
+
+    def select(g, perm, part):
+        start, size = part.start, part.size
+        width = cut(size, 1408)
+
+        @pl.loop(0, size // width)
         def _(i):
-            cols = pl.ds(pl.multiple_of(i * width, LANES), width)
+            cols = pl.ds(pl.multiple_of(start + i * width, LANES), width)
             got = jnp.dot(
                 perm, blk[pl.ds(32 * g, 32), cols], preferred_element_type=F32
             ).astype(BF)
@@ -200,7 +209,7 @@
                 Push(sel.at[g, r16(j - 1), cols], xin.at[r16(4 * g + j), cols], dev)
                 for j, dev in ((3, b_op), (1, b_up), (2, b_dn))
             ]
-            for cols in (pl.ds(0, D), pl.ds(D, D + LANES))
+            for cols in parts_in
         ]
 
     sent = [dispatch(0), dispatch(1)]
@@ -223,54 +232,54 @@
         for i in range(PIECES)
     ]
 
-    gather[0].wait()
-    select(0)
-    go(sent[0][0] + sent[0][1])
-    arrived(gather[1:])
-    select(1)
-    go(sent[1][0] + sent[1][1])
+    for g in range(2):
+        mine = (lambda k: [gather[k][0]]) if g == 0 else (lambda k: gather[k][1:])
+        arrived(mine(0))
+        perm = selection(g)
+        select(g, perm, parts_in[0])
+        go(sent[g][0])
+        arrived(mine(1))
+        select(g, perm, parts_in[1])
+        go(sent[g][1])
     place = [placing(0), placing(1)]
 
     for c in loads[2:]:
         c.wait()
     arrived(halves)
-    depth = 512 if D % 512 == 0 else LANES
+    tall = 2 * W
 
     def experts(g):
         rows = pl.ds(64 * g, 64)
-        acc[...] = jnp.zeros((64, 4 * W), F32)
-        acd[...] = jnp.zeros((64, 2 * W), F32)
         arrived(sent[g][0])
 
-        @pl.loop(0, D // depth)
+        @pl.loop(0, 2)
         def _(k):
-            cols = pl.ds(pl.multiple_of(k * depth, LANES), depth)
-            acc[...] += dot_nt(xin[rows, cols], w1[:, cols])
+            units = pl.ds(pl.multiple_of(k * tall, tall), tall)
+            acc[units] = dot_nt(w1[units], xin[rows, pl.ds(LANES, D)])
 
         arrived(sent[g][1])
-
-        @pl.loop(0, D // depth)
-        def _(k):
-            cols = pl.ds(pl.multiple_of(k * depth, LANES), depth)
-            cols_d = pl.ds(pl.multiple_of(D + k * depth, LANES), depth)
-            acd[...] += dot_nt(xin[rows, cols_d], w2[:, cols])
-
-        gate_pre = acc[:, 0 : 2 * W]
-        up_pre = acc[:, 2 * W : 4 * W]
-        hidden = acd[...]
-        lane = iota((64, LANES), 1)
-        gate = jnp.sum(
-            jnp.where(lane == own_e, xin[rows, pl.ds(2 * D, LANES)].astype(F32), 0.0),
-            axis=1, keepdims=True,
-        )
+        hidden = dot_nt(w2[...], xin[rows, pl.ds(LANES + D, D)])
+        gate_pre = acc[0:tall]
+        up_pre = acc[tall : 2 * tall]
+        chosen = ones(iota((16, LANES), 1) == own_e)
+        gate = dot_nt(chosen, xin[rows, head])[0:1]
         sig = jax.nn.sigmoid(gate_pre)
         act = gate_pre * sig
         slope = sig * (1.0 + gate_pre * (1.0 - sig))
-        score = jnp.sum(act * up_pre * hidden, axis=1, keepdims=True)
+        score = jnp.sum(act * up_pre * hidden, axis=0, keepdims=True)
         scaled = hidden * gate
         grads = jnp.concatenate(
-            [(scaled * up_pre * slope).astype(BF), (scaled * act).astype(BF)], axis=1
-        )
+            [
+                jnp.transpose(scaled * up_pre * slope).astype(BF),
+                jnp.transpose(scaled * act).astype(BF),
+            ],
+            axis=1,
+        )
+        score = jnp.sum(
+            jnp.where(iota((64, 64), 0) == iota((64, 64), 1), score, 0.0),
+            axis=1, keepdims=True,
+        )
+        lane = iota((64, LANES), 1)
         scores = resplit(jnp.where((lane % 64) == own_e, score, 0.0))
         rr[r16(4 * g), side] = scores[0:16]
         res[g, :, side] = scores[16:64]
@@ -363,8 +372,7 @@
             pltpu.VMEM((128, wide), BF),
             pltpu.VMEM((4 * W, D), BF),
             pltpu.VMEM((2 * W, D), BF),
-            pltpu.VMEM((64, 4 * W), F32),
-            pltpu.VMEM((64, 2 * W), F32),
+            pltpu.VMEM((4 * W, 64), F32),
             pltpu.VMEM((2, 48, back), BF),
             pltpu.VMEM((128, back), BF),
             pltpu.VMEM((48, back), BF),

time: 57 us -> 52.9 us (0.928)
  the two profiles are of different devices: /device:TPU:2 before, /device:TPU:8 now
where the time goes in v3:
time: 52.9 us; the launch traced here: 52.7 us
  Pallas kernels  49.3 us (93%)
  local copies, waits for them, and re-layouts  2.8 us (5%)
  between operations  0.64 us (1%)
    pallas_call x1, Pallas kernels, on_device(): pl.pallas_call(kernel, out_shape=(jax.ShapeDtypeStruct(tokens_in.shape, B...  49.3 us
    unnamed x2, local copies, waits for them, and re-layouts  2.8 us

profile of v3, /device:TPU:8, one launch (start us, length us, event | category | flops | bytes accessed | tf_op | source)
XLA Modules:
  0.0 52.7 jit_solution(4216459567101078868)
XLA Ops:
  0.6 49.3 %shard_map.86 = (bf16[1,16,4096]{2,1,0:T(8,128)(2,1)}, f32[1,2,16]{2,1,0:T(2,128)}) custom-call(bf16[1,16,4096]{2,1,0:T(8,128)(2,1)} %x_in.1, bf16[1,16,4096]{2,1,0:T(8,128)(2,1)} %dy_in.1, s32[1,2,16]{2,1,0:T(2,128)} %bitcast.4, bf16[1,2,16]{2,1,0:T(2,128)(2,1)} %bitcast.5, bf16[1,192,4096]{2,1,0:T(8,128)(2,1)} %wg_in.1, bf16[1,192,4096]{2,1,0:T(8,128)(2,1)} %wu_in.1, ...), custom_call_target="tpu_custom_call" | custom-call | tf_op jit(solution)/shard_map/pallas_call | solution.py:361
  49.9 1.6 %copy.11 = bf16[1,16,4096]{2,1,0:T(8,128)(2,1)} copy(bf16[1,16,4096]{2,1,0:T(8,128)(2,1)} %get-tuple-element.8) | data formatting | bytes 262144
  51.5 1.2 %copy.12 = f32[1,16,2]{1,2,0:T(2,128)} copy(f32[1,16,2]{1,2,0:T(2,128)} %bitcast.3) | data formatting | bytes 256

commit v4 on v3

--- a/solution.py
+++ b/solution.py
@@ -37,7 +37,7 @@
 def kernel(
     x_in, dy_in, ids_in, gw_in, wg_in, wu_in, wd_in, out, route,
     blk, sel, xin, w1, w2, acc, res, rr, tb, own, parts, fin,
-    send, recv, local,
+    ids_v, gates_v, route_v, send, recv, local,
 ):
     D = x_in.shape[2]
     W = wg_in.shape[1]
@@ -112,10 +112,17 @@
         pl.ds(i * step, step + (LANES if i == PIECES - 1 else 0)) for i in range(PIECES)
     ]
 
+    barrier = pltpu.get_barrier_semaphore()
+    around = (a_up, a_dn, a_op, b_up, b_dn, b_op, sib, z_dn, z_up)
+    for dev in around:
+        pl.semaphore_signal(barrier, inc=1, device_id=dev, device_id_type=MESH)
+
     loads = [
         pltpu.make_async_copy(s, d, local.at[i])
         for i, (s, d) in enumerate(
             [
+                (ids_in.at[0], ids_v),
+                (gw_in.at[0], gates_v),
                 (x_in.at[0], blk.at[r16(0), pl.ds(LANES, D)]),
                 (dy_in.at[0], blk.at[r16(0), pl.ds(LANES + D, D)]),
                 (wg_in.at[0], w1.at[pl.ds(0, W)]),
@@ -127,13 +134,10 @@
     for c in loads:
         c.start()
 
-    barrier = pltpu.get_barrier_semaphore()
-    around = (a_up, a_dn, a_op, b_up, b_dn, b_op, sib, z_dn, z_up)
-    for dev in around:
-        pl.semaphore_signal(barrier, inc=1, device_id=dev, device_id_type=MESH)
-
-    ids = ids_in[0]
-    gates = gw_in[0].astype(F32)
+    loads[0].wait()
+    loads[1].wait()
+    ids = ids_v[...]
+    gates = gates_v[...].astype(F32)
     eye = ones(iota((16, 16), 0) == iota((16, 16), 1))
     row_e = iota((LANES, 16), 0)
     table = jnp.zeros((LANES, 16), F32)
@@ -142,7 +146,7 @@
     blk[r16(0), head] = dot_nt(eye, table.astype(BF)).astype(BF)
 
     pl.semaphore_wait(barrier, len(around))
-    loads[0].wait()
+    loads[2].wait()
 
     gather = [
         [
@@ -152,7 +156,7 @@
         for cols in parts_in
     ]
     go(gather[0][:2])
-    loads[1].wait()
+    loads[3].wait()
     go(gather[1][:2] + [gather[0][2], gather[1][2]])
     halves = [
         Push(wg_in.at[0], w1.at[pl.ds(W, W)], sib),
@@ -243,7 +247,7 @@
         go(sent[g][1])
     place = [placing(0), placing(1)]
 
-    for c in loads[2:]:
+    for c in loads[4:]:
         c.wait()
     arrived(halves)
     tall = 2 * W
@@ -344,19 +348,33 @@
         col = jnp.sum(
             jnp.where(lane16 == ids_col[:, k : k + 1], got, 0.0), axis=1, keepdims=True
         )
-        route[0, k : k + 1, :] = jnp.sum(
+        route_v[k : k + 1, :] = jnp.sum(
             jnp.where(iota((16, 16), 0) == iota((16, 16), 1), col, 0.0),
             axis=0, keepdims=True,
         )
+    route_out = pltpu.make_async_copy(route_v, route.at[0], local.at[7])
+    route_out.start()
     finish()
+    route_out.wait()
+
+
+def hand_on(grad_in, route_in, grad_out, route_out, done):
+    copies = [
+        pltpu.make_async_copy(grad_in, grad_out, done.at[0]),
+        pltpu.make_async_copy(route_in, route_out, done.at[1]),
+    ]
+    for c in copies:
+        c.start()
+    for c in copies:
+        c.wait()
 
 
 def on_device(tokens_in, out_grad, expert_ids, gate_weights, w_gate, w_up, w_down):
     D = tokens_in.shape[2]
     W = w_gate.shape[1]
     wide, back = 2 * D + LANES, D + LANES
-    hbm = pl.BlockSpec(memory_space=pl.ANY)
-    vmem = pl.BlockSpec(memory_space=pltpu.VMEM)
+    anywhere = pl.BlockSpec(memory_space=pl.ANY)
+    hbm = pl.BlockSpec(memory_space=pltpu.HBM)
     ids = jnp.swapaxes(expert_ids, 1, 2)
     grad, route = pl.pallas_call(
         kernel,
@@ -364,8 +382,8 @@
             jax.ShapeDtypeStruct(tokens_in.shape, BF),
             jax.ShapeDtypeStruct(ids.shape, F32),
         ),
-        in_specs=[hbm, hbm, vmem, vmem, hbm, hbm, hbm],
-        out_specs=(hbm, vmem),
+        in_specs=[hbm] * 7,
+        out_specs=(anywhere, anywhere),
         scratch_shapes=[
             pltpu.VMEM((64, wide), BF),
             pltpu.VMEM((2, 48, wide), BF),
@@ -379,12 +397,36 @@
             pltpu.VMEM((16, back), F32),
             pltpu.VMEM((3, 16, back), BF),
             pltpu.VMEM((16, D), BF),
+            pltpu.VMEM((2, 16), jnp.int32),
+            pltpu.VMEM((2, 16), BF),
+            pltpu.VMEM((2, 16), F32),
             pltpu.SemaphoreType.DMA((COPIES,)),
             pltpu.SemaphoreType.DMA((COPIES,)),
-            pltpu.SemaphoreType.DMA((5,)),
+            pltpu.SemaphoreType.DMA((8,)),
         ],
-        compiler_params=pltpu.CompilerParams(collective_id=0, has_side_effects=True),
-    )(tokens_in, out_grad, ids, jnp.swapaxes(gate_weights, 1, 2), w_gate, w_up, w_down)
+        compiler_params=pltpu.CompilerParams(
+            collective_id=0, has_side_effects=True, vmem_limit_bytes=24 << 20
+        ),
+    )(
+        *(
+            pltpu.with_memory_space_constraint(v, pltpu.HBM)
+            for v in (
+                tokens_in, out_grad, ids, jnp.swapaxes(gate_weights, 1, 2),
+                w_gate, w_up, w_down,
+            )
+        )
+    )
+    grad, route = pl.pallas_call(
+        hand_on,
+        out_shape=(
+            jax.ShapeDtypeStruct(grad.shape, BF),
+            jax.ShapeDtypeStruct(route.shape, F32),
+        ),
+        in_specs=[anywhere] * 2,
+        out_specs=(hbm, hbm),
+        scratch_shapes=[pltpu.SemaphoreType.DMA((2,))],
+        compiler_params=pltpu.CompilerParams(vmem_limit_bytes=4 << 20),
+    )(grad, route)
     return grad, jnp.swapaxes(route, 1, 2)
 
 

time: 52.9 us -> 49.6 us (0.938)
  local copies, waits for them, and re-layouts: 2.8 us -> 0 us
    unnamed x2 -> x0, local copies, waits for them, and re-layouts: 2.8 us -> none
    pallas_call x1, Pallas kernels: 49.3 us -> 48.2 us  [on_device(): pl.pallas_call(kernel, out_shape=(jax.ShapeDtypeStruct(tokens_in.shape, B...]
    pallas_call x0 -> x1, Pallas kernels: none -> 0.68 us  [on_device(): pl.pallas_call(hand_on, out_shape=(jax.ShapeDtypeStruct(grad.shape, BF),...]
where the time goes in v4:
time: 49.6 us; the launch traced here: 49.5 us
  Pallas kernels  48.8 us (98%)
  between operations  0.64 us (1%)
    pallas_call x1, Pallas kernels, on_device(): pl.pallas_call(kernel, out_shape=(jax.ShapeDtypeStruct(tokens_in.shape, B...  48.2 us

profile of v4, /device:TPU:8, one launch (start us, length us, event | category | flops | bytes accessed | tf_op | source)
XLA Modules:
  0.0 49.5 jit_solution(3362406280544022508)
XLA Ops:
  0.6 48.2 %shard_map.86 = (bf16[1,16,4096]{2,1,0:T(8,128)(2,1)S(1)}, f32[1,2,16]{2,1,0:T(2,128)S(1)}) custom-call(bf16[1,16,4096]{2,1,0:T(8,128)(2,1)} %x_in.1, bf16[1,16,4096]{2,1,0:T(8,128)(2,1)} %dy_in.1, s32[1,2,16]{2,1,0:T(2,128)} %bitcast.3, bf16[1,2,16]{2,1,0:T(2,128)(2,1)} %bitcast.4, bf16[1,192,4096]{2,1,0:T(8,128)(2,1)} %wg_in.1, ...), custom_call_target="tpu_custom_call" | custom-call | tf_op jit(solution)/shard_map/pallas_call | solution.py:379
  48.8 0.7 %shard_map.87 = (bf16[1,16,4096]{2,1,0:T(8,128)(2,1)}, f32[1,2,16]{2,1,0:T(2,128)}) custom-call(bf16[1,16,4096]{2,1,0:T(8,128)(2,1)S(1)} %get-tuple-element.6.grad_in, f32[1,2,16]{2,1,0:T(2,128)S(1)} %get-tuple-element.7.route_in), custom_call_target="tpu_custom_call" | custom-call | tf_op jit(solution)/shard_map/pallas_call | solution.py:419

commit v5 on v4

--- a/solution.py
+++ b/solution.py
@@ -211,7 +211,7 @@
         return [
             [
                 Push(sel.at[g, r16(j - 1), cols], xin.at[r16(4 * g + j), cols], dev)
-                for j, dev in ((3, b_op), (1, b_up), (2, b_dn))
+                for j, dev in ((1, b_up), (2, b_dn), (3, b_op))
             ]
             for cols in parts_in
         ]

time: 49.6 us -> 49.6 us (level)
  the two profiles are of different devices: /device:TPU:8 before, /device:TPU:2 now
where the time goes in v5:
time: 49.6 us; the launch traced here: 49.4 us
  Pallas kernels  48.8 us (98%)
  between operations  0.64 us (1%)
    pallas_call x1, Pallas kernels, on_device(): pl.pallas_call(kernel, out_shape=(jax.ShapeDtypeStruct(tokens_in.shape, B...  48.1 us

profile of v5, /device:TPU:2, one launch (start us, length us, event | category | flops | bytes accessed | tf_op | source)
XLA Modules:
  0.0 49.4 jit_solution(11257418965943207180)
XLA Ops:
  0.6 48.1 %shard_map.86 = (bf16[1,16,4096]{2,1,0:T(8,128)(2,1)S(1)}, f32[1,2,16]{2,1,0:T(2,128)S(1)}) custom-call(bf16[1,16,4096]{2,1,0:T(8,128)(2,1)} %x_in.1, bf16[1,16,4096]{2,1,0:T(8,128)(2,1)} %dy_in.1, s32[1,2,16]{2,1,0:T(2,128)} %bitcast.3, bf16[1,2,16]{2,1,0:T(2,128)(2,1)} %bitcast.4, bf16[1,192,4096]{2,1,0:T(8,128)(2,1)} %wg_in.1, ...), custom_call_target="tpu_custom_call" | custom-call | tf_op jit(solution)/shard_map/pallas_call | solution.py:379
  48.8 0.7 %shard_map.87 = (bf16[1,16,4096]{2,1,0:T(8,128)(2,1)}, f32[1,2,16]{2,1,0:T(2,128)}) custom-call(bf16[1,16,4096]{2,1,0:T(8,128)(2,1)S(1)} %get-tuple-element.6.grad_in, f32[1,2,16]{2,1,0:T(2,128)S(1)} %get-tuple-element.7.route_in), custom_call_target="tpu_custom_call" | custom-call | tf_op jit(solution)/shard_map/pallas_call | solution.py:419
